TPU v7x, 512 devices: a whole 4x8x8 slice. The times are simulated.
512 devices in a mesh: section: 16 (over x, z_hi), tensor: 32 (over y, z_lo, core).
Axes of the slice: x: 4, y: 8, z: 8 (z_hi: 4, z_lo: 2; z = z_hi * 2 + z_lo), core: 2. Of those that a mesh axis runs over, the one named last changes fastest.
Arguments:
- x_in: bfloat16 [16, 512, 4096], P('section', 'tensor'), may hold values from -40 to 40
- grad_out: bfloat16 [16, 512, 4096], P('section', 'tensor'), may hold values from -50 to 50
- gain: float32 [16, 4096], P('section'), may hold values from 0.5 to 1.5
- w_val: bfloat16 [16, 4096, 4096], P('section', 'tensor'), may hold values from -0.09375 to 0.09375
- w_out: bfloat16 [16, 4096, 4096], P('section', 'tensor'), may hold values from -0.09375 to 0.09375
- filt: float32 [16, 3, 4096], P('section', None, 'tensor'), may hold values from -3 to 3
- tail: bfloat16 [16, 2, 4096], P('section', None, 'tensor'), may hold values from -6 to 6
- micro_index: int32 [16], P('section'), may hold values from 0 to 15
Outputs:
- grad_in: bfloat16 [16, 512, 4096], P('section', 'tensor')
- grad_w_val: bfloat16 [16, 4096, 4096], P('section', 'tensor')
- grad_w_out: bfloat16 [16, 4096, 4096], P('section', 'tensor')
- grad_filter: float32 [16, 3, 4096], P('section', None, 'tensor')
- grad_tail: float32 [16, 2, 4096], P('section', None, 'tensor')
- grad_gain: float32 [16, 4096], P('section')
All inputs are finite; a program needn't handle non-finite values.
Results may differ from a plain program's by a relative error of at most 0.023.
Values may be sent and summed in bfloat16 or wider, within the bound.
No kernel may reach another device: no remote copies, remote signals or barrier semaphores. Data moves between devices by JAX's collectives and lax.ppermute only.
A program may use at most 64 MiB of HBM per device.

v0:
```python
import jax
import jax.numpy as jnp
from jax import lax
from jax.sharding import PartitionSpec as P

TAPS = 3
EPSILON = 1e-06


def shifted(block, axis, distance):
    devices = range(lax.axis_size(axis))
    route = [((i - distance) % len(devices), i) for i in devices]
    return lax.ppermute(block, axis, route)


def contract_last(left, right):
    return lax.dot_general(
        left, right, (((1,), (1,)), ((), ())), preferred_element_type=jnp.float32
    )


def contract_first(left, right):
    return lax.dot_general(
        left, right, (((0,), (0,)), ((), ())), preferred_element_type=jnp.float32
    )


def on_device(x_in, grad_out, gain, w_val, w_out, filt, tail, micro_index):
    x_rows = x_in[0]
    cot_rows = grad_out[0]
    gain_row = gain[0]
    val_weight = w_val[0]
    out_weight = w_out[0]
    filters = filt[0]
    tail_rows = tail[0]
    has_tail = micro_index[0] > 0
    x_float = x_rows.astype(jnp.float32)
    inv_rms = lax.rsqrt(jnp.mean(x_float * x_float, axis=-1, keepdims=True) + EPSILON)
    normed = (x_float * inv_rms * gain_row).astype(jnp.bfloat16)
    normed_all = lax.all_gather(normed, "tensor", axis=0, tiled=True)
    seq_len = normed_all.shape[0]
    values = contract_last(normed_all, val_weight).astype(jnp.bfloat16)
    lead_rows = jnp.where(has_tail, tail_rows, jnp.zeros_like(tail_rows))
    extended = jnp.concatenate([lead_rows, values], axis=0).astype(jnp.float32)
    conv_out = filters[0] * extended[TAPS - 1 : TAPS - 1 + seq_len]
    for tap in range(1, TAPS):
        conv_out = conv_out + filters[tap] * extended[TAPS - 1 - tap : TAPS - 1 - tap + seq_len]
    gate_sig = jax.nn.sigmoid(conv_out)
    gated = (conv_out * gate_sig).astype(jnp.bfloat16)
    grad_gated = contract_last(lax.all_gather(cot_rows, "tensor", axis=0, tiled=True), out_weight)
    grad_wo = contract_first(gated, lax.all_gather(cot_rows, "tensor", axis=0, tiled=True))
    grad_conv = grad_gated * gate_sig * (1.0 + conv_out * (1.0 - gate_sig))
    grad_filter = jnp.stack(
        [
            jnp.sum(grad_conv * extended[TAPS - 1 - tap : TAPS - 1 - tap + seq_len], axis=0)
            for tap in range(TAPS)
        ]
    )
    padded = jnp.pad(grad_conv, ((TAPS - 1, TAPS - 1), (0, 0)))
    grad_ext = filters[0] * padded[0 : seq_len + TAPS - 1]
    for tap in range(1, TAPS):
        grad_ext = grad_ext + filters[tap] * padded[tap : tap + seq_len + TAPS - 1]
    grad_values = grad_ext[TAPS - 1 :].astype(jnp.bfloat16)
    grad_tail = jnp.where(has_tail, grad_ext[: TAPS - 1], jnp.zeros_like(grad_ext[: TAPS - 1]))
    grad_wv = contract_first(grad_values, normed_all)
    grad_normed = lax.psum_scatter(
        jnp.dot(grad_values, val_weight, preferred_element_type=jnp.float32).astype(jnp.bfloat16),
        "tensor",
        scatter_dimension=0,
        tiled=True,
    ).astype(jnp.float32)
    gain_term = jnp.sum(grad_normed * x_float * inv_rms, axis=0)
    grad_gain = lax.psum(gain_term, "tensor")
    scaled = gain_row * grad_normed
    grad_local = (
        cot_rows.astype(jnp.float32)
        + inv_rms * scaled
        - x_float * inv_rms**3 * jnp.mean(scaled * x_float, axis=-1, keepdims=True)
    )
    received = shifted(grad_local.astype(jnp.bfloat16), "section", -1)
    return (
        received[None],
        grad_wv.astype(jnp.bfloat16)[None],
        grad_wo.astype(jnp.bfloat16)[None],
        grad_filter[None],
        grad_tail[None],
        grad_gain[None],
    )


def solution(mesh):
    placed = (
        P("section", "tensor", None),
        P("section", "tensor", None),
        P("section", None),
        P("section", "tensor", None),
        P("section", "tensor", None),
        P("section", None, "tensor"),
        P("section", None, "tensor"),
        P("section"),
    )
    return jax.shard_map(
        on_device,
        mesh=mesh,
        in_specs=placed,
        out_specs=(
            P("section", "tensor", None),
            P("section", "tensor", None),
            P("section", "tensor", None),
            P("section", None, "tensor"),
            P("section", None, "tensor"),
            P("section", None),
        ),
        check_vma=False,
    )
```

profile of v0, /device:TPU:32, one launch (start us, length us, event | category | flops | bytes accessed | tf_op | source)
XLA Modules:
  0.0 413.5 jit_solution(13749967059140600081)
XLA Ops:
  7.2 1.2 fusion.18
  8.4 1.7 fusion.20
  10.1 0.0 all-gather.6.cloned.1.call-start
  10.2 0.7 all-gather.6.cloned.1.call-update
  10.9 0.0 reduce-scatter.2.cloned.1.call-start
  11.6 0.7 fusion.27
  12.2 0.7 slice_bitcast_fusion.2
  12.9 69.8 %all-gather.4.cloned.1.call-done = bf16[512,4096]{1,0:T(8,128)(2,1)} async-done(((bf16[16,4096]{1,0:T(8,128)(2,1)}), bf16[512,4096]{1,0:T(8,128)(2,1)}) %all-gather.4.cloned.1.call-update) | async-done | bytes 4194320 | tf_op jit(solution)/shard_map/all_gather | solution.py:40
  82.7 3.4 convolution_convert_fusion.3
  86.2 0.1 multiply_add_fusion.1
  86.3 67.6 %all-gather.6.cloned.1.call-done = bf16[1,512,4096]{2,1,0:T(8,128)(2,1)} async-done(((bf16[1,16,4096]{2,1,0:T(8,128)(2,1)}), bf16[1,512,4096]{2,1,0:T(8,128)(2,1)}) %all-gather.6.cloned.1.call-update) | async-done | bytes 4194320 | tf_op jit(solution)/shard_map/all_gather | solution.py:50
  153.9 3.5 multiply_reduce_fusion.2
  157.4 0.1 multiply_add_fusion
  157.5 3.2 convolution_convert_fusion
  160.8 0.6 copy.14
  161.4 4.2 %fusion.1 = bf16[1,128,4096]{2,1,0:T(8,128)(2,1)} fusion(bf16[1,512,4096]{2,1,0:T(8,128)(2,1)} %all-gather.6.cloned.1.call-done, f32[512,128]{1,0:T(8,128)S(1)} %multiply_add_fusion.1), kind=kOutput, calls=%fused_computation.4 | convolution fusion | flops 537722880 | bytes 5505024 | tf_op jit(solution)/shard_map/dot_general | solution.py:23
  165.6 1.7 fusion
  167.3 120.2 %reduce-scatter.2.cloned.1.call-done = bf16[16,4096]{1,0:T(8,128)(2,1)} async-done(((bf16[512,4096]{1,0:T(8,128)(2,1)}), bf16[16,4096]{1,0:T(8,128)(2,1)}) %reduce-scatter.2.cloned.1.call-update) | async-done | bytes 131088 | tf_op jit(solution)/shard_map/reduce_scatter | solution.py:66
  287.6 1.2 fusion.24
  288.7 1.0 fusion.17
  289.8 7.5 %collective-permute-start = (bf16[16,4096]{1,0:T(8,128)(2,1)S(1)}, bf16[16,4096]{1,0:T(8,128)(2,1)S(1)}, u32[]{:S(2)}, u32[]{:S(2)}) collective-permute-start(bf16[16,4096]{1,0:T(8,128)(2,1)S(1)} %fusion.17), channel_id=1, source_target_pairs={{32,0},{64,32},{96,64},{128,96},{160,128},{192,160},{224,192},{256... | collective-permute-start | bytes 393224 | tf_op jit(solution)/shard_map/ppermute | solution.py:13
  297.3 0.6 fusion.26
  297.9 108.5 %psum.7 = f32[1,4096]{1,0:T(1,128)} all-reduce(f32[1,4096]{1,0:T(1,128)S(1)} %bitcast.60), channel_id=1, replica_groups=mesh['section'=16,'tensor'=32] {'tensor'}, use_global_device_ids=true, to_apply=%region_7.8 | all-reduce | flops 4096 | bytes 32768 | tf_op jit(solution)/shard_map/psum | solution.py:73
  406.3 0.7 copy.17
  (20 shorter events, 0.2 us)
Async XLA Ops:
  7.2 75.6 %copy-start = (bf16[1,128,4096]{2,1,0:T(8,128)(2,1)S(1)}, bf16[1,128,4096]{2,1,0:T(8,128)(2,1)}, u32[]{:S(2)}) copy-start(bf16[1,128,4096]{2,1,0:T(8,128)(2,1)} %param.11) | copy-start | bytes 3145732
  7.2 146.8 %copy-start.5 = (bf16[1,128,4096]{2,1,0:T(8,128)(2,1)S(1)}, bf16[1,128,4096]{2,1,0:T(8,128)(2,1)}, u32[]{:S(2)}) copy-start(bf16[1,128,4096]{2,1,0:T(8,128)(2,1)} %param.12) | copy-start | bytes 3145732
  7.2 75.5 %all-gather.4.cloned.1.call-start = ((), (), s32[]{:S(2)}) async-start(), calls=%async_computation.1 | async-start | bytes 4325376 | tf_op jit(solution)/shard_map/all_gather | solution.py:40
  10.1 143.8 %all-gather.6.cloned.1.call-start = ((), (), s32[]{:S(2)}) async-start(), calls=%async_computation.3 | async-start | bytes 4325376 | tf_op jit(solution)/shard_map/all_gather | solution.py:50
  10.9 276.7 %reduce-scatter.2.cloned.1.call-start = ((), (), s32[]{:S(2)}) async-start(), calls=%async_computation.2 | async-start | bytes 4325376 | tf_op jit(solution)/shard_map/reduce_scatter | solution.py:66
  160.8 4.8 %copy-start.1 = (bf16[512,4096]{1,0:T(8,128)(2,1)S(1)}, bf16[512,4096]{1,0:T(8,128)(2,1)}, u32[]{:S(2)}) copy-start(bf16[512,4096]{1,0:T(8,128)(2,1)} %all-gather.4.cloned.1.call-done) | copy-start | bytes 12582916
  161.3 126.2 %copy-start.2 = (bf16[1,16,4096]{2,1,0:T(8,128)(2,1)S(1)}, bf16[1,16,4096]{2,1,0:T(8,128)(2,1)}, u32[]{:S(2)}) copy-start(bf16[1,16,4096]{2,1,0:T(8,128)(2,1)} %param.8) | copy-start | bytes 393220
  161.3 126.2 %copy-start.4 = (f32[1,4096]{1,0:T(1,128)S(1)}, f32[1,4096]{1,0:T(1,128)}, u32[]{:S(2)}) copy-start(f32[1,4096]{1,0:T(1,128)} %param.10) | copy-start | bytes 49156
  165.6 123.1 %copy-start.3 = (bf16[1,16,4096]{2,1,0:T(8,128)(2,1)S(1)}, bf16[1,16,4096]{2,1,0:T(8,128)(2,1)}, u32[]{:S(2)}) copy-start(bf16[1,16,4096]{2,1,0:T(8,128)(2,1)} %param.9) | copy-start | bytes 393220
  289.8 116.6 %collective-permute-start = (bf16[16,4096]{1,0:T(8,128)(2,1)S(1)}, bf16[16,4096]{1,0:T(8,128)(2,1)S(1)}, u32[]{:S(2)}, u32[]{:S(2)}) collective-permute-start(bf16[16,4096]{1,0:T(8,128)(2,1)S(1)} %fusion.17), channel_id=1, source_target_pairs={{32,0},{64,32},{96,64},{128,96},{160,128},{192,160},{224,192},{256... | collective-permute-start | bytes 393224 | tf_op jit(solution)/shard_map/ppermute | solution.py:13
Sparse Core Ops, SparseCore 0:
  10.7 71.9 all-gather.3
  84.9 69.0 all-gather.5
  160.9 126.6 reduce-scatter.1
where the time goes:
time: 414 us
  waiting for transfers between devices  258 us (62%)
  blocking collectives  108 us (26%)
  matrix products  16.1 us (4%)
  between operations  14.5 us (4%)
  starting transfers between devices  7.63 us (2%)
  other arithmetic  6.52 us (2%)
    reduce_scatter x1, waiting for transfers between devices, on_device(): lax.psum_scatter(jnp.dot(grad_values, val_weight, preferred_element_type=...  120 us
    psum x1, blocking collectives, on_device(): grad_gain = lax.psum(gain_term, 'tensor')  108 us
    all_gather x1, waiting for transfers between devices, on_device(): normed_all = lax.all_gather(normed, 'tensor', axis=0, tiled=True)  69.8 us
    all_gather x1, waiting for transfers between devices, on_device(): lax.all_gather(cot_rows, 'tensor', axis=0, tiled=True)  67.6 us
  transfers between devices with their start and end apart: 4, of which 3 were waited for; matrix products, arithmetic and copies ran while one was open for 3% of the time, Pallas kernels for 0%

commit v1 on v0

--- a/solution.py
+++ b/solution.py
@@ -47,7 +47,12 @@
         conv_out = conv_out + filters[tap] * extended[TAPS - 1 - tap : TAPS - 1 - tap + seq_len]
     gate_sig = jax.nn.sigmoid(conv_out)
     gated = (conv_out * gate_sig).astype(jnp.bfloat16)
-    grad_gated = contract_last(lax.all_gather(cot_rows, "tensor", axis=0, tiled=True), out_weight)
+    grad_gated = contract_last(
+        jnp.concatenate(
+            lax.all_to_all(jnp.stack([cot_rows] * lax.axis_size("tensor")), "tensor", 0, 0), axis=0
+        ),
+        out_weight,
+    )
     grad_wo = contract_first(gated, lax.all_gather(cot_rows, "tensor", axis=0, tiled=True))
     grad_conv = grad_gated * gate_sig * (1.0 + conv_out * (1.0 - gate_sig))
     grad_filter = jnp.stack(

time: 414 us -> 453 us (1.094)
  waiting for transfers between devices: 258 us -> 283 us
  starting transfers between devices: 7.63 us -> 18.2 us
    all_gather x1, waiting for transfers between devices: 69.8 us -> 98.3 us  [on_device(): normed_all = lax.all_gather(normed, 'tensor', axis=0, tiled=True)]
    all_gather x1, waiting for transfers between devices: 67.6 us -> 52.1 us  [on_device(): lax.all_gather(cot_rows, 'tensor', axis=0, tiled=True)]
    all_to_all x0 -> x1, starting transfers between devices: none -> 10.1 us  [on_device(): lax.all_to_all(jnp.stack([cot_rows] * lax.axis_size('tensor')), 'tensor',...]
    all_to_all x0 -> x1, waiting for transfers between devices: none -> 6.65 us  [on_device(): lax.all_to_all(jnp.stack([cot_rows] * lax.axis_size('tensor')), 'tensor',...]
    reduce_scatter x1, waiting for transfers between devices: 120 us -> 126 us  [on_device(): lax.psum_scatter(jnp.dot(grad_values, val_weight, preferred_element_type=...]
  transfers between devices with their start and end apart: 4 -> 5, of which waited for: 3 -> 4; matrix products, arithmetic and copies ran while one was open for 3% -> 5% of each run, Pallas kernels for 0% -> 0%
where the time goes in v1:
time: 453 us; the launch traced here: 452 us
  waiting for transfers between devices  283 us (62%)
  blocking collectives  108 us (24%)
  starting transfers between devices  18.2 us (4%)
  matrix products  18 us (4%)
  between operations  14.5 us (3%)
  other arithmetic  5.8 us (1%)
  local copies, waits for them, and re-layouts  4.63 us (1%)
    reduce_scatter x1, waiting for transfers between devices, on_device(): lax.psum_scatter(jnp.dot(grad_values, val_weight, preferred_element_type=...  126 us
    psum x1, blocking collectives, on_device(): grad_gain = lax.psum(gain_term, 'tensor')  108 us
    all_gather x1, waiting for transfers between devices, on_device(): normed_all = lax.all_gather(normed, 'tensor', axis=0, tiled=True)  98.3 us
    all_gather x1, waiting for transfers between devices, on_device(): lax.all_gather(cot_rows, 'tensor', axis=0, tiled=True)  52.1 us
    all_to_all x1, starting transfers between devices, on_device(): lax.all_to_all(jnp.stack([cot_rows] * lax.axis_size('tensor')), 'tensor',...  10.1 us
  transfers between devices with their start and end apart: 5, of which 4 were waited for; matrix products, arithmetic and copies ran while one was open for 5% of the time, Pallas kernels for 0%

profile of v1, /device:TPU:32, one launch (start us, length us, event | category | flops | bytes accessed | tf_op | source)
XLA Modules:
  0.0 452.3 jit_solution(11367107334244772959)
XLA Ops:
  7.2 1.1 fusion.11
  8.4 1.7 fusion.13
  10.1 3.4 stack.15
  13.4 10.1 %all-to-all-start = ((bf16[32,16,4096]{2,1,0:T(8,128)(2,1)}), bf16[32,16,4096]{2,1,0:T(8,128)(2,1)}, u32[]{:S(2)}, u32[]{:S(2)}) async-start(bf16[32,16,4096]{2,1,0:T(8,128)(2,1)} %stack.15), calls=%async_computation | async-start | bytes 8388608 | tf_op jit(solution)/shard_map/all_to_all | solution.py:52
  23.6 0.0 all-gather.6.cloned.1.call-start
  23.6 0.7 all-gather.6.cloned.1.call-update
  25.1 98.3 %all-gather.4.cloned.1.call-done = bf16[512,4096]{1,0:T(8,128)(2,1)} async-done(((bf16[16,4096]{1,0:T(8,128)(2,1)}), bf16[512,4096]{1,0:T(8,128)(2,1)}) %all-gather.4.cloned.1.call-update) | async-done | bytes 4194320 | tf_op jit(solution)/shard_map/all_gather | solution.py:40
  123.4 3.4 convolution_convert_fusion.3
  126.8 0.1 multiply_add_fusion.1
  126.9 6.6 %all-to-all-done = bf16[32,16,4096]{2,1,0:T(8,128)(2,1)} async-done(((bf16[32,16,4096]{2,1,0:T(8,128)(2,1)}), bf16[32,16,4096]{2,1,0:T(8,128)(2,1)}, u32[]{:S(2)}, u32[]{:S(2)}) %all-to-all-start) | async-done | bytes 4194336 | tf_op jit(solution)/shard_map/all_to_all | solution.py:52
  133.6 3.5 multiply_reduce_fusion.2
  137.1 0.1 multiply_add_fusion
  137.2 3.2 convolution_convert_fusion
  140.4 0.6 copy.14
  141.0 3.9 fusion
  144.9 52.1 %all-gather.6.cloned.1.call-done = bf16[1,512,4096]{2,1,0:T(8,128)(2,1)} async-done(((bf16[1,16,4096]{2,1,0:T(8,128)(2,1)}), bf16[1,512,4096]{2,1,0:T(8,128)(2,1)}) %all-gather.6.cloned.1.call-update) | async-done | bytes 4194320 | tf_op jit(solution)/shard_map/all_gather | solution.py:56
  197.0 3.9 fusion.1
  200.9 125.6 %reduce-scatter.2.cloned.1.call-done = bf16[16,4096]{1,0:T(8,128)(2,1)} async-done(((bf16[512,4096]{1,0:T(8,128)(2,1)}), bf16[16,4096]{1,0:T(8,128)(2,1)}) %reduce-scatter.2.cloned.1.call-update) | async-done | bytes 131088 | tf_op jit(solution)/shard_map/reduce_scatter | solution.py:71
  326.6 1.2 fusion.17
  327.8 1.0 fusion.10
  328.8 7.9 %collective-permute-start = (bf16[16,4096]{1,0:T(8,128)(2,1)S(1)}, bf16[16,4096]{1,0:T(8,128)(2,1)S(1)}, u32[]{:S(2)}, u32[]{:S(2)}) collective-permute-start(bf16[16,4096]{1,0:T(8,128)(2,1)S(1)} %fusion.10), channel_id=1, source_target_pairs={{32,0},{64,32},{96,64},{128,96},{160,128},{192,160},{224,192},{256... | collective-permute-start | bytes 393224 | tf_op jit(solution)/shard_map/ppermute | solution.py:13
  336.7 0.6 fusion.19
  337.3 107.8 %psum.7 = f32[1,4096]{1,0:T(1,128)} all-reduce(f32[1,4096]{1,0:T(1,128)S(1)} %bitcast.54), channel_id=1, replica_groups=mesh['section'=16,'tensor'=32] {'tensor'}, use_global_device_ids=true, to_apply=%region_7.8 | all-reduce | flops 4096 | bytes 32768 | tf_op jit(solution)/shard_map/psum | solution.py:78
  445.1 0.7 copy.17
  (25 shorter events, 0.2 us)
Async XLA Ops:
  7.2 116.2 %copy-start = (bf16[1,128,4096]{2,1,0:T(8,128)(2,1)S(1)}, bf16[1,128,4096]{2,1,0:T(8,128)(2,1)}, u32[]{:S(2)}) copy-start(bf16[1,128,4096]{2,1,0:T(8,128)(2,1)} %param.11) | copy-start | bytes 3145732
  7.2 116.2 %all-gather.4.cloned.1.call-start = ((), (), s32[]{:S(2)}) async-start(), calls=%async_computation.2 | async-start | bytes 4325376 | tf_op jit(solution)/shard_map/all_gather | solution.py:40
  13.4 11.6 %copy-start.6 = (bf16[1,2,128]{2,1,0:T(2,128)(2,1)S(1)}, bf16[1,2,128]{2,1,0:T(2,128)(2,1)}, u32[]{:S(2)}) copy-start(bf16[1,2,128]{2,1,0:T(2,128)(2,1)} %param.14) | copy-start | bytes 1540
  13.4 11.6 %copy-start.4 = (f32[1,3,128]{2,0,1:T(1,128)S(1)}, f32[1,3,128]{2,0,1:T(1,128)}, u32[]{:S(2)}) copy-start(f32[1,3,128]{2,0,1:T(1,128)} %param.13) | copy-start | bytes 4612
  13.4 120.1 %all-to-all-start = ((bf16[32,16,4096]{2,1,0:T(8,128)(2,1)}), bf16[32,16,4096]{2,1,0:T(8,128)(2,1)}, u32[]{:S(2)}, u32[]{:S(2)}) async-start(bf16[32,16,4096]{2,1,0:T(8,128)(2,1)} %stack.15), calls=%async_computation | async-start | bytes 8388608 | tf_op jit(solution)/shard_map/all_to_all | solution.py:52
  23.6 110.0 %copy-start.5 = (bf16[1,128,4096]{2,1,0:T(8,128)(2,1)S(1)}, bf16[1,128,4096]{2,1,0:T(8,128)(2,1)}, u32[]{:S(2)}) copy-start(bf16[1,128,4096]{2,1,0:T(8,128)(2,1)} %param.12) | copy-start | bytes 3145732
  23.6 173.4 %all-gather.6.cloned.1.call-start = ((), (), s32[]{:S(2)}) async-start(), calls=%async_computation.4 | async-start | bytes 4325376 | tf_op jit(solution)/shard_map/all_gather | solution.py:56
  24.3 302.2 %reduce-scatter.2.cloned.1.call-start = ((), (), s32[]{:S(2)}) async-start(), calls=%async_computation.3 | async-start | bytes 4325376 | tf_op jit(solution)/shard_map/reduce_scatter | solution.py:71
  141.0 185.6 %copy-start.1 = (bf16[1,16,4096]{2,1,0:T(8,128)(2,1)S(1)}, bf16[1,16,4096]{2,1,0:T(8,128)(2,1)}, u32[]{:S(2)}) copy-start(bf16[1,16,4096]{2,1,0:T(8,128)(2,1)} %param.8) | copy-start | bytes 393220
  141.0 185.6 %copy-start.3 = (f32[1,4096]{1,0:T(1,128)S(1)}, f32[1,4096]{1,0:T(1,128)}, u32[]{:S(2)}) copy-start(f32[1,4096]{1,0:T(1,128)} %param.10) | copy-start | bytes 49156
  144.9 182.8 %copy-start.2 = (bf16[1,16,4096]{2,1,0:T(8,128)(2,1)S(1)}, bf16[1,16,4096]{2,1,0:T(8,128)(2,1)}, u32[]{:S(2)}) copy-start(bf16[1,16,4096]{2,1,0:T(8,128)(2,1)} %param.9) | copy-start | bytes 393220
  328.8 116.3 %collective-permute-start = (bf16[16,4096]{1,0:T(8,128)(2,1)S(1)}, bf16[16,4096]{1,0:T(8,128)(2,1)S(1)}, u32[]{:S(2)}, u32[]{:S(2)}) collective-permute-start(bf16[16,4096]{1,0:T(8,128)(2,1)S(1)} %fusion.10), channel_id=1, source_target_pairs={{32,0},{64,32},{96,64},{128,96},{160,128},{192,160},{224,192},{256... | collective-permute-start | bytes 393224 | tf_op jit(solution)/shard_map/ppermute | solution.py:13
Sparse Core Ops, SparseCore 0:
  10.7 112.5 all-gather.3
  125.5 71.4 all-gather.5
  199.8 126.7 reduce-scatter.1
